TPU v7x, 512 devices: a whole 4x8x8 slice. The times are simulated.
512 devices in a mesh: wide: 64 (over y, z), narrow: 8 (over x, core).
Axes of the slice: x: 4, y: 8, z: 8, core: 2. Of those that a mesh axis runs over, the one named last changes fastest.
Arguments:
- cand_ids: int32 [128, 32768], P(None, ('wide', 'narrow')), may hold values from 0 to 59999
- cand_request: int32 [32768], P(('wide', 'narrow')), may hold values from 0 to 7
- tables: bfloat16 [128, 1024, 256], P('wide'), may hold values from -4 to 4
- table_rows: int32 [128], P('wide'), may hold values from 256 to 1024
- width_choice: int32 [128], P('wide'), may hold values from 0 to 3
- projections: bfloat16 [128, 256, 128], P('wide'), may hold values from -0.5 to 0.5
- user_dense: bfloat16 [512, 512], P(('wide', 'narrow')), may hold values from -6 to 6
- user_weight: bfloat16 [512, 1024], replicated, may hold values from -0.25 to 0.25
- cross_down: bfloat16 [2048, 256], P('narrow'), may hold values from -0.125 to 0.125
- cross_up: bfloat16 [256, 2048], P(None, 'narrow'), may hold values from -0.375 to 0.375
- cross_bias: float32 [2048], replicated, may hold values from -3 to 3
- deep_in: bfloat16 [2048, 512], P('narrow'), may hold values from -0.125 to 0.125
- deep_mid: bfloat16 [512, 256], replicated, may hold values from -0.25 to 0.25
- head_cross: float32 [2048], replicated, may hold values from -0.125 to 0.125
- head_deep: float32 [256], replicated, may hold values from -0.375 to 0.375
Outputs:
- crossed: bfloat16 [32768, 2048], P(('wide', 'narrow'))
- scores: float32 [32768], P(('wide', 'narrow'))
All inputs are finite; a program needn't handle non-finite values.
Results may differ from a plain program's by a relative error of at most 0.0072.
Values may be sent and summed in bfloat16 or wider, within the bound.
No kernel may reach another device: no remote copies, remote signals or barrier semaphores. Data moves between devices by JAX's collectives and lax.ppermute only.
A program may use at most 64 MiB of HBM per device.

v0:
```python
import jax
import jax.numpy as jnp
from jax import lax
from jax.sharding import PartitionSpec as P

SLOTS = 8


def per_device(
    cand_ids,
    cand_request,
    tables,
    table_rows,
    width_choice,
    projections,
    user_dense,
    user_weight,
    cross_down,
    cross_up,
    cross_bias,
    deep_in,
    deep_mid,
    head_cross,
    head_deep,
):
    nwide = lax.axis_size("wide")
    tab_dev = tables.shape[0]
    emb_width = tables.shape[2]
    rows_dev = cand_request.shape[0]
    columns = jnp.arange(emb_width, dtype=jnp.int32)

    def width_mask(t):
        width = jnp.left_shift(jnp.int32(32), width_choice[t])
        return columns < width

    projected = [
        jnp.dot(
            jnp.where(width_mask(t)[None, :], tables[t], jnp.zeros((), jnp.bfloat16)),
            projections[t],
            preferred_element_type=jnp.float32,
        ).astype(jnp.bfloat16)
        for t in range(tab_dev)
    ]
    feature_ids = cand_ids.reshape(nwide, tab_dev, rows_dev)
    received = lax.all_to_all(feature_ids, "wide", split_axis=0, concat_axis=0, tiled=True)
    results = []
    for t in range(tab_dev):
        index = jnp.remainder(received[:, t, :], table_rows[t])
        results.append(jnp.take(projected[t], index, axis=0))
    stacked = jnp.stack(results, axis=1)
    pooled = jnp.sum(stacked, axis=1, keepdims=True, dtype=jnp.float32).astype(jnp.bfloat16)
    returned = lax.all_to_all(pooled, "wide", split_axis=0, concat_axis=0, tiled=True)
    owners = jnp.sum(returned, axis=1, dtype=jnp.float32).astype(jnp.bfloat16)
    slots = jnp.sum(
        owners.reshape(nwide // SLOTS, SLOTS, rows_dev, owners.shape[2]), axis=0, dtype=jnp.float32
    ).astype(jnp.bfloat16)
    item = slots.transpose(1, 0, 2).reshape(rows_dev, SLOTS * owners.shape[2])
    mine = jax.nn.silu(jnp.dot(user_dense, user_weight, preferred_element_type=jnp.float32)).astype(
        jnp.bfloat16
    )
    users = lax.all_gather(mine, "narrow", axis=0, tiled=True)
    req_count = users.shape[0]
    selector = (cand_request[:, None] == jnp.arange(req_count, dtype=jnp.int32)[None, :]).astype(
        jnp.bfloat16
    )
    user_part = jnp.dot(selector, users, preferred_element_type=jnp.float32).astype(jnp.bfloat16)
    x0 = jnp.concatenate([user_part, item], axis=1)
    low_sum = jnp.dot(
        x0,
        lax.all_gather(cross_down, "narrow", axis=0, tiled=True),
        preferred_element_type=jnp.float32,
    )
    deep_sum = jnp.dot(
        x0,
        lax.all_gather(deep_in, "narrow", axis=0, tiled=True),
        preferred_element_type=jnp.float32,
    )
    low = low_sum.astype(jnp.bfloat16)
    deep = jax.nn.relu(deep_sum).astype(jnp.bfloat16)
    upward = jnp.dot(
        low,
        lax.all_gather(cross_up, "narrow", axis=1, tiled=True),
        preferred_element_type=jnp.float32,
    )
    base = x0.astype(jnp.float32)
    crossed = (base * (upward + cross_bias) + base).astype(jnp.bfloat16)
    hidden = jax.nn.relu(jnp.dot(deep, deep_mid, preferred_element_type=jnp.float32))
    scores = jnp.dot(crossed.astype(jnp.float32), head_cross, precision=lax.Precision.HIGHEST)
    scores = scores + jnp.dot(hidden, head_deep, precision=lax.Precision.HIGHEST)
    return (crossed, scores)


def solution(mesh):
    return jax.shard_map(
        per_device,
        mesh=mesh,
        in_specs=(
            P(None, ("wide", "narrow")),
            P(("wide", "narrow")),
            P("wide", None, None),
            P("wide"),
            P("wide"),
            P("wide", None, None),
            P(("wide", "narrow"), None),
            P(),
            P("narrow", None),
            P(None, "narrow"),
            P(),
            P("narrow", None),
            P(),
            P(),
            P(),
        ),
        out_specs=(P(("wide", "narrow"), None), P(("wide", "narrow"))),
        check_vma=False,
    )
```

profile of v0, /device:TPU:6, one launch (start us, length us, event | category | flops | bytes accessed | tf_op | source)
XLA Modules:
  0.0 127.5 jit_solution(469522532853063279)
XLA Ops:
  7.3 0.7 all-gather.5.cloned.1.call-update
  8.0 0.7 all-gather.7.cloned.1.call-update
  8.7 0.8 copy.21
  9.6 0.7 reshape.113
  10.3 16.6 %all-to-all-start = ((s32[64,1,128]{2,1,0:T(1,128)}), s32[64,1,128]{2,1,0:T(1,128)S(1)}, u32[]{:S(2)}, u32[]{:S(2)}) async-start(s32[64,1,128]{2,1,0:T(1,128)} %reshape.113), calls=%async_computation | async-start | bytes 65536 | tf_op jit(solution)/shard_map/all_to_all | solution.py:45
  26.9 0.7 all-gather.9.cloned.1.call-update
  27.6 1.4 %fusion.32 = (s32[1]{0:T(128)}, s32[1]{0:T(128)}) fusion(s32[2]{0:T(128)} %param.21), kind=kLoop, calls=%fused_computation.59 | loop fusion | bytes 16 | tf_op jit(solution)/shard_map/slice | solution.py:33
  30.4 1.3 %convolution_convert_fusion.1 = bf16[1024,128]{1,0:T(8,128)(2,1)S(1)} fusion(bf16[2,1024,256]{2,1,0:T(8,128)(2,1)} %param.19, pred[256]{0:T(512)(128)(4,1)S(1)} %iota_compare_fusion.3, bf16[2,256,128]{2,1,0:T(8,128)(2,1)} %param.22), kind=kOutput, calls=%fused_computation.7 | convolution fusion | flops 67502080 | bytes 852224 | tf_op jit(solution)/shard_map/dot_general | solution.py:37
  31.7 0.3 convolution_convert_fusion
  32.1 0.7 fusion.31
  35.4 3.4 %all-to-all-done = s32[64,1,128]{2,1,0:T(1,128)S(1)} async-done(((s32[64,1,128]{2,1,0:T(1,128)}), s32[64,1,128]{2,1,0:T(1,128)S(1)}, u32[]{:S(2)}, u32[]{:S(2)}) %all-to-all-start) | async-done | bytes 32800 | tf_op jit(solution)/shard_map/all_to_all | solution.py:45
  38.8 0.5 broadcast.42
  39.3 0.7 reduce.4
  40.1 4.9 %slice_remainder_fusion.1 = (s32[64,1,64]{2,1,0:T(1,128)S(1)}, s32[64,1,64]{2,1,0:T(1,128)S(1)}) fusion(s32[64,2,64]{2,1,0:T(2,128)S(1)} %reshape.114, s32[]{:T(128)S(6)} %select_n.37, s32[]{:T(128)S(6)} %select_n.41), kind=kLoop, calls=%fused_computation.41 | loop fusion | flops 8192 | bytes 65544 | tf_op jit(solution)/shard_map/jit(remainder)/rem | solution.py:48
  45.2 12.1 %gather_fusion = bf16[4096,128]{1,0:T(8,128)(2,1)S(1)} fusion(bf16[1024,128]{1,0:T(8,128)(2,1)S(1)} %convolution_convert_fusion.1, s32[4096]{0:T(1024)S(1)} %broadcast_clamp_fusion.1), kind=kCustom, calls=%fused_computation.clone | custom fusion | bytes 2113536 | tf_op jit(solution)/shard_map/jit(_take)/gather | solution.py:49
  57.4 15.0 %gather_fusion.1 = bf16[4096,128]{1,0:T(8,128)(2,1)} fusion(bf16[1024,128]{1,0:T(8,128)(2,1)S(1)} %convolution_convert_fusion, s32[4096]{0:T(1024)S(1)} %broadcast_clamp_fusion), kind=kCustom, calls=%fused_computation.1.clone | custom fusion | bytes 2113536 | tf_op jit(solution)/shard_map/jit(_take)/gather | solution.py:49
  72.4 4.0 %fusion.5 = bf16[64,1,64,128]{3,2,1,0:T(8,128)(2,1)} fusion(bf16[64,64,128]{2,1,0:T(8,128)(2,1)} %bitcast.55, bf16[64,64,128]{2,1,0:T(8,128)(2,1)S(1)} %bitcast.54, pred[64,64]{1,0:T(8,128)(4,1)S(1)} %get-tuple-element.5, pred[64,64]{1,0:T(8,128)(4,1)S(1)} %get-tuple-element.13), kind=kLoop, calls=%fused_computation.18 | loop fusion | flops 1572864 | bytes 3153920 | tf_op jit(solution)/shard_map/convert_element_type | solution.py:51
  76.5 9.5 %all-to-all-start.1 = ((bf16[64,1,64,128]{3,2,1,0:T(8,128)(2,1)}), bf16[64,1,64,128]{3,2,1,0:T(8,128)(2,1)S(1)}, u32[]{:S(2)}, u32[]{:S(2)}) async-start(bf16[64,1,64,128]{3,2,1,0:T(8,128)(2,1)} %fusion.5), calls=%async_computation.1 | async-start | bytes 2097152 | tf_op jit(solution)/shard_map/all_to_all | solution.py:52
  86.3 11.0 %all-gather = bf16[8192]{0:T(1024)(128)(2,1)S(1)} all-gather(bf16[1024]{0:T(1024)(128)(2,1)S(1)} %multiply_convert_fusion), channel_id=2, replica_groups=mesh['wide'=64,'narrow'=8] {'narrow'}, dimensions={0}, use_global_device_ids=true | all-gather | bytes 18432 | tf_op jit(solution)/shard_map/all_gather | solution.py:61
  97.5 17.6 %all-to-all-done.1 = bf16[64,1,64,128]{3,2,1,0:T(8,128)(2,1)S(1)} async-done(((bf16[64,1,64,128]{3,2,1,0:T(8,128)(2,1)}), bf16[64,1,64,128]{3,2,1,0:T(8,128)(2,1)S(1)}, u32[]{:S(2)}, u32[]{:S(2)}) %all-to-all-start.1) | async-done | bytes 1048608 | tf_op jit(solution)/shard_map/all_to_all | solution.py:52
  115.4 2.3 %fusion.2 = bf16[64,2048]{1,0:T(8,128)(2,1)S(1)} fusion(bf16[256,2048]{1,0:T(8,128)(2,1)} %all-gather.7.cloned.1.call-done, bf16[2048,256]{1,0:T(8,128)(2,1)} %all-gather.5.cloned.1.call-done, f32[2048]{0:T(1024)S(1)} %copy-done.3, bf16[64,1024]{1,0:T(8,128)(2,1)S(1)} %copy_bitcast_fusion, bf16[64,1024]{1,0:T(8,128)(2,1)S(1)} %convolution_convert_fusion.2), kind=kOutput, calls=%fused_computation.5 | convolution fusion | flops 135806976 | bytes 2629632 | tf_op jit(solution)/shard_map/dot_general | solution.py:80
  117.8 0.3 convolution_bitcast_fusion.1
  118.1 2.2 %convolution_maximum_fusion.1 = f32[64,256]{1,0:T(8,128)S(1)} fusion(bf16[512,256]{1,0:T(8,128)(2,1)S(1)} %copy-done.1, bf16[2048,512]{1,0:T(8,128)(2,1)} %all-gather.9.cloned.1.call-done, bf16[64,1024]{1,0:T(8,128)(2,1)S(1)} %copy_bitcast_fusion, bf16[64,1024]{1,0:T(8,128)(2,1)S(1)} %convolution_convert_fusion.2), kind=kOutput, calls=%fused_computation.11 | convolution fusion | flops 151601152 | bytes 2686976 | tf_op jit(solution)/shard_map/dot_general | solution.py:87
  120.3 0.7 fusion.4
  (42 shorter events, 1.2 us)
Async XLA Ops:
  7.2 78.9 %copy-start = (bf16[512,1024]{1,0:T(8,128)(2,1)S(1)}, bf16[512,1024]{1,0:T(8,128)(2,1)}, u32[]{:S(2)}) copy-start(bf16[512,1024]{1,0:T(8,128)(2,1)} %param.24) | copy-start | bytes 3145732
  7.2 24.6 %copy-start.8 = (bf16[2,1024,256]{2,1,0:T(8,128)(2,1)S(1)}, bf16[2,1024,256]{2,1,0:T(8,128)(2,1)}, u32[]{:S(2)}) copy-start(bf16[2,1024,256]{2,1,0:T(8,128)(2,1)} %param.19) | copy-start | bytes 3145732
  7.2 24.6 %copy-start.9 = (bf16[2,256,128]{2,1,0:T(8,128)(2,1)S(1)}, bf16[2,256,128]{2,1,0:T(8,128)(2,1)}, u32[]{:S(2)}) copy-start(bf16[2,256,128]{2,1,0:T(8,128)(2,1)} %param.22) | copy-start | bytes 393220
  7.2 24.8 %copy-start.5 = (s32[2]{0:T(128)S(1)}, s32[2]{0:T(128)}, u32[]{:S(2)}) copy-start(s32[2]{0:T(128)} %param.20) | copy-start | bytes 28
  7.2 108.1 %all-gather.5.cloned.1.call-start = ((), (), s32[]{:S(2)}) async-start(), calls=%async_computation.2 | async-start | bytes 1179648 | tf_op jit(solution)/shard_map/all_gather | solution.py:70
  7.9 107.4 %all-gather.7.cloned.1.call-start = ((), (), s32[]{:S(2)}) async-start(), calls=%async_computation.3 | async-start | bytes 1179648 | tf_op jit(solution)/shard_map/all_gather | solution.py:82
  10.3 28.5 %all-to-all-start = ((s32[64,1,128]{2,1,0:T(1,128)}), s32[64,1,128]{2,1,0:T(1,128)S(1)}, u32[]{:S(2)}, u32[]{:S(2)}) async-start(s32[64,1,128]{2,1,0:T(1,128)} %reshape.113), calls=%async_computation | async-start | bytes 65536 | tf_op jit(solution)/shard_map/all_to_all | solution.py:45
  26.9 91.2 %all-gather.9.cloned.1.call-start = ((), (), s32[]{:S(2)}) async-start(), calls=%async_computation.4 | async-start | bytes 2359296 | tf_op jit(solution)/shard_map/all_gather | solution.py:75
  72.4 13.6 %copy-start.4 = (bf16[1,512]{1,0:T(2,128)(2,1)S(1)}, bf16[1,512]{1,0:T(2,128)(2,1)}, u32[]{:S(2)}) copy-start(bf16[1,512]{1,0:T(2,128)(2,1)} %param.23) | copy-start | bytes 3076
  76.5 20.8 %copy-start.7 = (s32[64]{0:T(128)S(1)}, s32[64]{0:T(128)}, u32[]{:S(2)}) copy-start(s32[64]{0:T(128)} %param.18) | copy-start | bytes 772
  76.5 38.9 %copy-start.3 = (f32[2048]{0:T(1024)S(1)}, f32[2048]{0:T(1024)}, u32[]{:S(2)}) copy-start(f32[2048]{0:T(1024)} %param.27) | copy-start | bytes 24580
  76.5 38.7 %all-to-all-start.1 = ((bf16[64,1,64,128]{3,2,1,0:T(8,128)(2,1)}), bf16[64,1,64,128]{3,2,1,0:T(8,128)(2,1)S(1)}, u32[]{:S(2)}, u32[]{:S(2)}) async-start(bf16[64,1,64,128]{3,2,1,0:T(8,128)(2,1)} %fusion.5), calls=%async_computation.1 | async-start | bytes 2097152 | tf_op jit(solution)/shard_map/all_to_all | solution.py:52
  115.1 2.6 %copy-start.10 = (f32[2048]{0:T(1024)S(1)}, f32[2048]{0:T(1024)}, u32[]{:S(2)}) copy-start(f32[2048]{0:T(1024)} %param.30) | copy-start | bytes 24580
  115.1 3.0 %copy-start.1 = (bf16[512,256]{1,0:T(8,128)(2,1)S(1)}, bf16[512,256]{1,0:T(8,128)(2,1)}, u32[]{:S(2)}) copy-start(bf16[512,256]{1,0:T(8,128)(2,1)} %param.29) | copy-start | bytes 786436
  117.8 3.3 %copy-start.2 = (bf16[64,2048]{1,0:T(8,128)(2,1)}, bf16[64,2048]{1,0:T(8,128)(2,1)S(1)}, u32[]{:S(2)}) copy-start(bf16[64,2048]{1,0:T(8,128)(2,1)S(1)} %fusion.2) | copy-start | bytes 786436
  117.8 2.6 %copy-start.6 = (f32[256]{0:T(256)S(1)}, f32[256]{0:T(256)}, u32[]{:S(2)}) copy-start(f32[256]{0:T(256)} %param.31) | copy-start | bytes 3076
Sparse Core Ops, SparseCore 0:
  10.2 32.0 all-gather.4
  44.4 29.1 all-gather.6
  75.8 30.8 all-gather.8
where the time goes:
time: 129 us; the launch traced here: 128 us
  local copies, waits for them, and re-layouts  31.7 us (25%)
  starting transfers between devices  26.2 us (20%)
  waiting for transfers between devices  23.1 us (18%)
  between operations  18 us (14%)
  blocking collectives  11 us (9%)
  other arithmetic  9.92 us (8%)
  matrix products  7.65 us (6%)
    gather x2, local copies, waits for them, and re-layouts, per_device(): results.append(jnp.take(projected[t], index, axis=0))  27.2 us
    all_to_all x1, waiting for transfers between devices, per_device(): lax.all_to_all(pooled, 'wide', split_axis=0, concat_axis=0, tiled=True)  17.6 us
    all_to_all x1, starting transfers between devices, per_device(): lax.all_to_all(feature_ids, 'wide', split_axis=0, concat_axis=0, tiled=True)  16.6 us
    all_gather x1, blocking collectives, per_device(): users = lax.all_gather(mine, 'narrow', axis=0, tiled=True)  11 us
    all_to_all x1, starting transfers between devices, per_device(): lax.all_to_all(pooled, 'wide', split_axis=0, concat_axis=0, tiled=True)  9.53 us
    rem x1, other arithmetic, per_device(): index = jnp.remainder(received[:, t, :], table_rows[t])  4.92 us
    convert_element_type x1, other arithmetic, per_device(): jnp.sum(stacked, axis=1, keepdims=True, dtype=jnp.float32)  4.04 us
    all_to_all x1, waiting for transfers between devices, per_device(): lax.all_to_all(feature_ids, 'wide', split_axis=0, concat_axis=0, tiled=True)  3.36 us
  transfers between devices with their start and end apart: 5, of which 2 were waited for; matrix products, arithmetic and copies ran while one was open for 36% of the time, Pallas kernels for 0%

commit v1 on v0

v1 whole, which is shorter than its diff:
```python
import jax
import jax.numpy as jnp
from jax import lax
from jax.experimental import pallas as pl
from jax.experimental.pallas import tpu as pltpu
from jax.sharding import Mesh, PartitionSpec as P

F32 = jnp.float32
BF16 = jnp.bfloat16
CAND = 64
VOCAB = 1024
EMB = 256
PROJ = 128
SLOTS = 8
GROUPS = 4
PEERS = GROUPS * SLOTS
ROWS = PEERS * CAND
DENSE = 2048
HALF = 1024
RANK = 256
DEEP1 = 512
DEEP2 = 256
UIN = 512
PAYLOAD = 264
ANY = pl.ANY


def prep_kernel(
    scal, ids, tables, proj, user, down, deep, up,
    payload, ids_out, table_out,
    tab_buf, tr, urow, sems,
):
    copies = [
        pltpu.make_async_copy(tables, tab_buf, sems.at[0]),
        pltpu.make_async_copy(down, payload.at[pl.ds(0, 256), pl.ds(0, RANK)], sems.at[1]),
        pltpu.make_async_copy(deep, payload.at[pl.ds(0, 256), pl.ds(RANK, DEEP1)], sems.at[2]),
        pltpu.make_async_copy(up, payload.at[pl.ds(0, 256), pl.ds(RANK + DEEP1, 256)], sems.at[3]),
    ]
    for c in copies:
        c.start()
    urow[...] = jnp.zeros_like(urow)
    urow[0:1, 0:UIN] = user[...]
    last = pltpu.make_async_copy(urow, payload.at[pl.ds(256, 8), :], sems.at[4])
    last.start()
    tr[...] = jnp.transpose(ids[...])
    parity = scal[4]
    for j in range(GROUPS):
        pieces = []
        for p in range(2):
            base = j * 32 + p * 16
            first = tr[pl.ds(base, SLOTS, stride=2), :]
            second = tr[pl.ds(base + 1, SLOTS, stride=2), :]
            pieces.append(jnp.concatenate([first, second], axis=1))
        mine = jnp.where(parity == 0, pieces[0], pieces[1])
        other = jnp.where(parity == 0, pieces[1], pieces[0])
        ids_out[pl.ds(j * SLOTS, SLOTS), 0, :] = mine
        ids_out[pl.ds(j * SLOTS, SLOTS), 1, :] = other
    lane = lax.broadcasted_iota(jnp.int32, (8, PROJ), 1)
    sub = lax.broadcasted_iota(jnp.int32, (8, PROJ), 0)
    used = jnp.where(lane < CAND, scal[0], scal[1])
    parts = jnp.where(sub == 0, jnp.right_shift(used, 4), jnp.bitwise_and(used, 15))
    table_out[pl.ds(2 * VOCAB, 8), :] = parts.astype(F32).astype(BF16)
    copies[0].wait()
    row = lax.broadcasted_iota(jnp.int32, (EMB, PROJ), 0)
    for t in range(2):
        width = jnp.left_shift(jnp.int32(32), scal[2 + t])
        weight = jnp.where(row < width, proj[t].astype(F32), 0.0).astype(BF16)
        table_out[pl.ds(t * VOCAB, VOCAB), :] = jnp.dot(
            tab_buf[t], weight, preferred_element_type=F32
        ).astype(BF16)
    for c in copies[1:]:
        c.wait()
    last.wait()


def prep(scal, ids_t, tables, projections, user, down, deep, up):
    return pl.pallas_call(
        prep_kernel,
        out_shape=(
            jax.ShapeDtypeStruct((PAYLOAD, 1024), BF16),
            jax.ShapeDtypeStruct((PEERS, 2, 2 * CAND), jnp.int32),
            jax.ShapeDtypeStruct((2 * VOCAB + 8, PROJ), BF16),
        ),
        in_specs=[
            pl.BlockSpec(memory_space=pltpu.SMEM),
            pl.BlockSpec(memory_space=pltpu.VMEM),
            pl.BlockSpec(memory_space=ANY),
            pl.BlockSpec(memory_space=pltpu.VMEM),
            pl.BlockSpec(memory_space=pltpu.VMEM),
            pl.BlockSpec(memory_space=ANY),
            pl.BlockSpec(memory_space=ANY),
            pl.BlockSpec(memory_space=ANY),
        ],
        out_specs=(
            pl.BlockSpec(memory_space=ANY),
            pl.BlockSpec(memory_space=pltpu.VMEM),
            pl.BlockSpec(memory_space=pltpu.VMEM),
        ),
        scratch_shapes=[
            pltpu.VMEM((2, VOCAB, EMB), BF16),
            pltpu.VMEM((2 * CAND, CAND), jnp.int32),
            pltpu.VMEM((8, 1024), BF16),
            pltpu.SemaphoreType.DMA((5,)),
        ],
        name="prep",
    )(scal, ids_t, tables, projections, user, down, deep, up)


def lookup_kernel(ids, own, other, out):
    lows, highs = [], []
    for q, table in enumerate((own, other)):
        parts = table[pl.ds(2 * VOCAB, 8), :].astype(F32)
        used = parts[0:1, :] * 16.0 + parts[1:2, :]
        value = ids[:, q, :].astype(F32)
        quotient = jnp.floor(value / used)
        index = value - quotient * used
        index = jnp.where(index < 0.0, index + used, index)
        index = jnp.where(index >= used, index - used, index)
        high = jnp.floor(index * (1.0 / 256.0))
        lows.append(index - high * 256.0)
        highs.append(high)
    low = jnp.transpose(jnp.concatenate(lows, axis=0))
    high = jnp.transpose(jnp.concatenate(highs, axis=0))
    column = lax.broadcasted_iota(jnp.int32, (256, 256), 1).astype(F32)
    step = 256 // CAND
    for chunk in range(PEERS // step):
        acc = jnp.zeros((256, PROJ), F32)
        for q, table in enumerate((own, other)):
            for k in range(2):
                spots = [q * PEERS + chunk * step + s for s in range(step)]
                lo = jnp.concatenate([low[k * CAND:(k + 1) * CAND, s:s + 1] for s in spots], axis=0)
                hi = jnp.concatenate([high[k * CAND:(k + 1) * CAND, s:s + 1] for s in spots], axis=0)
                for h in range(VOCAB // 256):
                    hot = jnp.where(lo + hi * 256.0 == column + h * 256.0, 1.0, 0.0).astype(BF16)
                    acc = acc + jnp.dot(
                        hot, table[pl.ds(k * VOCAB + h * 256, 256), :], preferred_element_type=F32
                    )
        out[pl.ds(chunk * 256, 256), :] = acc.astype(BF16)


def lookup(ids, own, other):
    return pl.pallas_call(
        lookup_kernel,
        out_shape=jax.ShapeDtypeStruct((ROWS, PROJ), BF16),
        name="lookup",
    )(ids, own, other)


def user_kernel(request, weight, packed, chosen, partial, feats, w1, sems):
    copies = [pltpu.make_async_copy(packed.at[:, pl.ds(256, 8), pl.ds(0, UIN)], feats, sems.at[0])]
    for n in range(4):
        copies.append(
            pltpu.make_async_copy(
                packed.at[n, pl.ds(0, 256), pl.ds(0, RANK + DEEP1)],
                w1.at[pl.ds(n * 256, 256), :],
                sems.at[1 + n],
            )
        )
    for c in copies:
        c.start()
    copies[0].wait()
    dense = feats[...].astype(F32)[:, 0, :].astype(BF16)
    pre = jnp.dot(dense, weight[...], preferred_element_type=F32)
    users = (pre * (1.0 / (1.0 + jnp.exp(-pre)))).astype(BF16)
    select = lax.broadcasted_iota(jnp.int32, (SLOTS, CAND), 0) == request[...]
    mine = lax.dot_general(
        jnp.where(select, 1.0, 0.0).astype(BF16), users, (((0,), (0,)), ((), ())),
        preferred_element_type=F32,
    ).astype(BF16)
    chosen[...] = mine
    for c in copies[1:]:
        c.wait()
    partial[...] = jnp.dot(mine, w1[...], preferred_element_type=F32)


def user_part(request, weight, packed):
    return pl.pallas_call(
        user_kernel,
        out_shape=(
            jax.ShapeDtypeStruct((CAND, HALF), BF16),
            jax.ShapeDtypeStruct((CAND, RANK + DEEP1), F32),
        ),
        in_specs=[
            pl.BlockSpec(memory_space=pltpu.VMEM),
            pl.BlockSpec(memory_space=pltpu.VMEM),
            pl.BlockSpec(memory_space=ANY),
        ],
        scratch_shapes=[
            pltpu.VMEM((8, 8, UIN), BF16),
            pltpu.VMEM((HALF, RANK + DEEP1), BF16),
            pltpu.SemaphoreType.DMA((5,)),
        ],
        name="user_part",
    )(request, weight, packed)


def dense_kernel(
    returned, packed, chosen, partial, bias, mid, head_c, head_d,
    crossed_out, scores_out, w1, w2, sems,
):
    copies = []
    for n in range(4):
        copies.append(
            pltpu.make_async_copy(
                packed.at[4 + n, pl.ds(0, 256), pl.ds(0, RANK + DEEP1)],
                w1.at[pl.ds(n * 256, 256), :],
                sems.at[n],
            )
        )
    ups = [
        pltpu.make_async_copy(
            packed.at[n, pl.ds(0, 256), pl.ds(RANK + DEEP1, 256)], w2.at[n], sems.at[4 + n]
        )
        for n in range(8)
    ]
    for c in copies + ups:
        c.start()
    slots = []
    for s in range(SLOTS):
        total = returned[s].astype(F32)
        for g in range(1, GROUPS):
            total = total + returned[g * SLOTS + s].astype(F32)
        slots.append(total.astype(BF16))
    item = jnp.concatenate(slots, axis=1)
    for c in copies:
        c.wait()
    both = partial[...] + jnp.dot(item, w1[...], preferred_element_type=F32)
    low = both[:, :RANK].astype(BF16)
    deep = jnp.maximum(both[:, RANK:], 0.0).astype(BF16)
    hidden = jnp.maximum(jnp.dot(deep, mid[...], preferred_element_type=F32), 0.0)
    score = jnp.sum(hidden * head_d[...], axis=1, keepdims=True)
    for c in ups:
        c.wait()
    for n in range(8):
        cols = slice(n * 256, (n + 1) * 256)
        upward = jnp.dot(low, w2[n], preferred_element_type=F32)
        base = (chosen[:, cols] if n < 4 else item[:, n * 256 - HALF:(n + 1) * 256 - HALF]).astype(F32)
        cross = (base * (upward + bias[:, cols]) + base).astype(BF16)
        crossed_out[:, cols] = cross
        score = score + jnp.sum(cross.astype(F32) * head_c[:, cols], axis=1, keepdims=True)
    scores_out[...] = jnp.transpose(jnp.broadcast_to(score, (CAND, 128)))[0:1, :]


def dense_part(returned, packed, chosen, partial, bias, mid, head_c, head_d):
    vmem = pl.BlockSpec(memory_space=pltpu.VMEM)
    return pl.pallas_call(
        dense_kernel,
        out_shape=(
            jax.ShapeDtypeStruct((CAND, DENSE), BF16),
            jax.ShapeDtypeStruct((1, CAND), F32),
        ),
        in_specs=[vmem, pl.BlockSpec(memory_space=ANY)] + [vmem] * 6,
        scratch_shapes=[
            pltpu.VMEM((HALF, RANK + DEEP1), BF16),
            pltpu.VMEM((8, RANK, 256), BF16),
            pltpu.SemaphoreType.DMA((12,)),
        ],
        name="dense_part",
    )(returned, packed, chosen, partial, bias, mid, head_c, head_d)


def per_device(
    cand_ids,
    cand_request,
    tables,
    table_rows,
    width_choice,
    projections,
    user_dense,
    user_weight,
    cross_down,
    cross_up,
    cross_bias,
    deep_in,
    deep_mid,
    head_cross,
    head_deep,
):
    parity = lax.axis_index("yp").astype(jnp.int32)
    scal = jnp.concatenate([table_rows, width_choice, parity[None]])
    payload, ids_out, own = prep(
        scal, cand_ids.T, tables, projections, user_dense, cross_down, deep_in, cross_up
    )
    packed = lax.all_gather(payload, "narrow", axis=0, tiled=True).reshape(8, PAYLOAD, 1024)
    other = lax.ppermute(own, "yp", [(0, 1), (1, 0)])
    received = lax.all_to_all(ids_out, ("yj", "z"), split_axis=0, concat_axis=0, tiled=True)
    rows = lookup(received, own, other)
    returned = lax.all_to_all(
        rows.reshape(PEERS, CAND, PROJ), ("yj", "z"), split_axis=0, concat_axis=0, tiled=True
    )
    chosen, partial = user_part(cand_request.reshape(1, CAND), user_weight, packed)
    crossed, scores = dense_part(
        returned,
        packed,
        chosen,
        partial,
        cross_bias.reshape(1, DENSE),
        deep_mid,
        head_cross.reshape(1, DENSE),
        head_deep.reshape(1, DEEP2),
    )
    return crossed, scores.reshape(CAND)


def solution(mesh):
    inner = Mesh(mesh.devices.reshape(GROUPS, 2, SLOTS, 8), ("yj", "yp", "z", "narrow"))
    wide = ("yj", "yp", "z")
    everywhere = ("yj", "yp", "z", "narrow")
    return jax.shard_map(
        per_device,
        mesh=inner,
        in_specs=(
            P(None, everywhere),
            P(everywhere),
            P(wide, None, None),
            P(wide),
            P(wide),
            P(wide, None, None),
            P(everywhere, None),
            P(),
            P("narrow", None),
            P(None, "narrow"),
            P(),
            P("narrow", None),
            P(),
            P(),
            P(),
        ),
        out_specs=(P(everywhere, None), P(everywhere)),
        check_vma=False,
    )
```

time: 129 us -> 101 us (0.78)
  Pallas kernels: 0 us -> 33.9 us
  local copies, waits for them, and re-layouts: 31.7 us -> 1.62 us
  starting transfers between devices: 26.2 us -> 7.72 us
  blocking collectives: 11 us -> 27.4 us
  waiting for transfers between devices: 23.1 us -> 14 us
  other arithmetic: 9.92 us -> 1.28 us
  matrix products: 7.65 us -> 0 us
  between operations: 18 us -> 14.1 us
    pallas_call x0 -> x4, Pallas kernels: none -> 33.9 us  [the longest x1 18.8 us: prep(): pl.pallas_call(prep_kernel, out_shape=(jax.ShapeDtypeStruct((PAYLOAD, 102...]
    all_to_all x0 -> x1, blocking collectives: none -> 27.4 us  [per_device(): lax.all_to_all(ids_out, ('yj', 'z'), split_axis=0, concat_axis=0, tiled=T...]
    gather x2 -> x0, local copies, waits for them, and re-layouts: 27.2 us -> none  [per_device(): results.append(jnp.take(projected[t], index, axis=0))]
    all_to_all x2 -> x1, starting transfers between devices: 26.1 us -> 4.2 us  [per_device(): lax.all_to_all(rows.reshape(PEERS, CAND, PROJ), ('yj', 'z'), split_axis=0...]
    all_gather x1 -> x0, blocking collectives: 11 us -> none  [per_device(): users = lax.all_gather(mine, 'narrow', axis=0, tiled=True)]
    dot_general x8 -> x0, matrix products: 7.65 us -> none  [the longest x1 2.34 us: per_device(): jnp.dot(low, lax.all_gather(cross_up, 'narrow', axis=1, tiled=True), pref...]
    all_to_all x2 -> x1, waiting for transfers between devices: 21 us -> 14 us  [per_device(): lax.all_to_all(rows.reshape(PEERS, CAND, PROJ), ('yj', 'z'), split_axis=0...]
    rem x1 -> x0, other arithmetic: 4.92 us -> none  [per_device(): index = jnp.remainder(received[:, t, :], table_rows[t])]
  transfers between devices with their start and end apart: 5 -> 3, of which waited for: 2 -> 1; matrix products, arithmetic and copies ran while one was open for 36% -> 0% of each run, Pallas kernels for 0% -> 11%
where the time goes in v1:
time: 101 us; the launch traced here: 100 us
  Pallas kernels  33.9 us (34%)
  blocking collectives  27.4 us (27%)
  between operations  14.1 us (14%)
  waiting for transfers between devices  14 us (14%)
  starting transfers between devices  7.72 us (8%)
  local copies, waits for them, and re-layouts  1.62 us (2%)
  other arithmetic  1.28 us (1%)
    all_to_all x1, blocking collectives, per_device(): lax.all_to_all(ids_out, ('yj', 'z'), split_axis=0, concat_axis=0, tiled=T...  27.4 us
    pallas_call x1, Pallas kernels, prep(): pl.pallas_call(prep_kernel, out_shape=(jax.ShapeDtypeStruct((PAYLOAD, 102...  18.8 us
    all_to_all x1, waiting for transfers between devices, per_device(): lax.all_to_all(rows.reshape(PEERS, CAND, PROJ), ('yj', 'z'), split_axis=0...  14 us
    pallas_call x1, Pallas kernels, lookup(): pl.pallas_call(lookup_kernel, out_shape=jax.ShapeDtypeStruct((ROWS, PROJ)...  6.89 us
    pallas_call x1, Pallas kernels, dense_part(): pl.pallas_call(dense_kernel, out_shape=(jax.ShapeDtypeStruct((CAND, DENSE...  4.44 us
    all_to_all x1, starting transfers between devices, per_device(): lax.all_to_all(rows.reshape(PEERS, CAND, PROJ), ('yj', 'z'), split_axis=0...  4.2 us
    pallas_call x1, Pallas kernels, user_part(): pl.pallas_call(user_kernel, out_shape=(jax.ShapeDtypeStruct((CAND, HALF),...  3.81 us
    ppermute x1, starting transfers between devices, per_device(): other = lax.ppermute(own, 'yp', [(0, 1), (1, 0)])  3.48 us
  transfers between devices with their start and end apart: 3, of which 1 were waited for; matrix products, arithmetic and copies ran while one was open for 0% of the time, Pallas kernels for 11%

profile of v1, /device:TPU:6, one launch (start us, length us, event | category | flops | bytes accessed | tf_op | source)
XLA Modules:
  0.0 100.1 jit_solution(9390803542637810388)
XLA Ops:
  7.2 0.0 all-gather.2.cloned.1.call-start
  7.2 1.3 %pad_add_fusion.scal = s32[5]{0:T(128)} fusion(s32[1]{0:T(128)} %bitcast, s32[2]{0:T(128)} %param.19, s32[2]{0:T(128)} %param.18), kind=kLoop, calls=%fused_computation | loop fusion | flops 10 | bytes 40 | tf_op jit(solution)/shard_map/concatenate | solution.py:280
  8.5 18.8 %prep.1 = (bf16[264,1024]{1,0:T(8,128)(2,1)}, s32[32,2,128]{2,1,0:T(2,128)}, bf16[2056,128]{1,0:T(8,128)(2,1)}) custom-call(s32[5]{0:T(128)} %pad_add_fusion.scal, s32[64,128]{1,0:T(8,128)} %bitcast.12, bf16[2,1024,256]{2,1,0:T(8,128)(2,1)} %tables.1, bf16[2,256,128]{2,1,0:T(8,128)(2,1)} %proj.1, bf16[1,512]{1,0:T(2,128)(2,1)} %user.1, ...), custom_call_target="tpu_custom_call" | custom-call | tf_op jit(solution)/shard_map/prep/pallas_call | solution.py:77
  27.3 0.0 all-gather.2.cloned.1.call-update
  27.3 3.5 %collective-permute-start = (bf16[2056,128]{1,0:T(8,128)(2,1)}, bf16[2056,128]{1,0:T(8,128)(2,1)S(1)}, u32[]{:S(2)}, u32[]{:S(2)}) collective-permute-start(bf16[2056,128]{1,0:T(8,128)(2,1)} %get-tuple-element.10.own), channel_id=1, source_target_pairs={{0,64},{64,0},{1,65},{65,1},{2,66},{66,2},{3,67},{67,3},{4,68},{68... | collective-permute-start | bytes 1579016 | tf_op jit(solution)/shard_map/ppermute | solution.py:285
  30.8 27.4 %all_to_all.10.ids = s32[32,2,128]{2,1,0:T(2,128)} all-to-all(s32[32,2,128]{2,1,0:T(2,128)} %get-tuple-element.9), channel_id=1, replica_groups=mesh['yj'=4,'yp'=2,'z'=8,'narrow'=8] {'yj','z'}, dimensions={0} | all-to-all | bytes 65536 | tf_op jit(solution)/shard_map/all_to_all | solution.py:286
  58.2 0.0 collective-permute-done.other
  58.2 0.0 copy-start.1
  58.2 0.8 copy-done.1
  59.0 6.9 %lookup.1 = bf16[2048,128]{1,0:T(8,128)(2,1)} custom-call(s32[32,2,128]{2,1,0:T(2,128)} %all_to_all.10.ids, bf16[2056,128]{1,0:T(8,128)(2,1)} %get-tuple-element.10.own, bf16[2056,128]{1,0:T(8,128)(2,1)} %copy-done.1), custom_call_target="tpu_custom_call" | custom-call | tf_op jit(solution)/shard_map/lookup/pallas_call | solution.py:142
  65.9 4.2 %all-to-all-start.1 = ((bf16[32,64,128]{2,1,0:T(8,128)(2,1)}), bf16[32,64,128]{2,1,0:T(8,128)(2,1)S(1)}, u32[]{:S(2)}, u32[]{:S(2)}) async-start(bf16[32,64,128]{2,1,0:T(8,128)(2,1)} %bitcast.11), calls=%async_computation.1 | async-start | bytes 1048576 | tf_op jit(solution)/shard_map/all_to_all | solution.py:288
  70.1 0.0 all-gather.2.cloned.1.call-done
  70.2 3.8 %user_part.1 = (bf16[64,1024]{1,0:T(8,128)(2,1)}, f32[64,768]{1,0:T(8,128)}) custom-call(s32[1,64]{1,0:T(1,128)} %bitcast.16, bf16[512,1024]{1,0:T(8,128)(2,1)} %weight.1, bf16[8,264,1024]{2,1,0:T(8,128)(2,1)} %bitcast.9), custom_call_target="tpu_custom_call" | custom-call | tf_op jit(solution)/shard_map/user_part/pallas_call | solution.py:177
  74.0 14.0 %all-to-all-done.1.returned = bf16[32,64,128]{2,1,0:T(8,128)(2,1)S(1)} async-done(((bf16[32,64,128]{2,1,0:T(8,128)(2,1)}), bf16[32,64,128]{2,1,0:T(8,128)(2,1)S(1)}, u32[]{:S(2)}, u32[]{:S(2)}) %all-to-all-start.1) | async-done | bytes 524320 | tf_op jit(solution)/shard_map/all_to_all | solution.py:288
  88.0 0.0 copy-start
  88.0 0.8 copy-done
  88.8 4.4 %dense_part.1 = (bf16[64,2048]{1,0:T(8,128)(2,1)}, f32[1,64]{1,0:T(1,128)}) custom-call(bf16[32,64,128]{2,1,0:T(8,128)(2,1)} %copy-done, bf16[8,264,1024]{2,1,0:T(8,128)(2,1)} %bitcast.10, bf16[64,1024]{1,0:T(8,128)(2,1)} %get-tuple-element.12.chosen, f32[64,768]{1,0:T(8,128)} %get-tuple-element.13.partial, f32[1,2048]{1,0:T(1,128)} %bitcast.13, ...), custom_call_target="tpu_custom_call" | custom-call | tf_op jit(solution)/shard_map/dense_part/pallas_call | solution.py:246
Async XLA Ops:
  7.2 63.0 %all-gather.2.cloned.1.call-start = ((), (), s32[]{:S(2)}) async-start(), calls=%async_computation.2 | async-start | bytes 4866048 | tf_op jit(solution)/shard_map/all_gather | solution.py:284
  27.3 30.9 %collective-permute-start = (bf16[2056,128]{1,0:T(8,128)(2,1)}, bf16[2056,128]{1,0:T(8,128)(2,1)S(1)}, u32[]{:S(2)}, u32[]{:S(2)}) collective-permute-start(bf16[2056,128]{1,0:T(8,128)(2,1)} %get-tuple-element.10.own), channel_id=1, source_target_pairs={{0,64},{64,0},{1,65},{65,1},{2,66},{66,2},{3,67},{67,3},{4,68},{68... | collective-permute-start | bytes 1579016 | tf_op jit(solution)/shard_map/ppermute | solution.py:285
  58.2 0.8 copy-start.1
  65.9 22.0 %all-to-all-start.1 = ((bf16[32,64,128]{2,1,0:T(8,128)(2,1)}), bf16[32,64,128]{2,1,0:T(8,128)(2,1)S(1)}, u32[]{:S(2)}, u32[]{:S(2)}) async-start(bf16[32,64,128]{2,1,0:T(8,128)(2,1)} %bitcast.11), calls=%async_computation.1 | async-start | bytes 1048576 | tf_op jit(solution)/shard_map/all_to_all | solution.py:288
  88.0 0.8 copy-start
Sparse Core Ops, SparseCore 0:
  27.4 40.7 all-gather.1

commit v2 on v1

v2 whole, which is shorter than its diff:
```python
import jax
import jax.numpy as jnp
from jax import lax
from jax.experimental import pallas as pl
from jax.experimental.pallas import tpu as pltpu
from jax.sharding import Mesh, PartitionSpec as P

F32 = jnp.float32
BF16 = jnp.bfloat16
CAND = 64
VOCAB = 1024
EMB = 256
PROJ = 128
SLOTS = 8
GROUPS = 4
PEERS = GROUPS * SLOTS
ROWS = PEERS * CAND
DENSE = 2048
HALF = 1024
RANK = 256
DEEP1 = 512
DEEP2 = 256
UIN = 512
PAYLOAD = 264
ANY = pl.ANY


def in_vmem(x):
    return pltpu.with_memory_space_constraint(x, pltpu.VMEM)


def prep_kernel(
    rows, widths, ids, tables, proj, user, down, deep, up,
    ids_out, table_out, payload,
    tab_buf, tr, packed, sems,
):
    core = lax.axis_index("c")
    parity = lax.axis_index("yp")
    loads = [
        pltpu.make_async_copy(down, packed.at[pl.ds(0, 256), pl.ds(0, RANK)], sems.at[0]),
        pltpu.make_async_copy(deep, packed.at[pl.ds(0, 256), pl.ds(RANK, DEEP1)], sems.at[1]),
        pltpu.make_async_copy(up, packed.at[pl.ds(0, 256), pl.ds(RANK + DEEP1, 256)], sems.at[2]),
        pltpu.make_async_copy(tables.at[core], tab_buf, sems.at[3]),
    ]
    for c in loads:
        c.start()
    packed[pl.ds(256, 8), :] = jnp.zeros((8, 1024), BF16)
    packed[pl.ds(256, 1), pl.ds(0, UIN)] = user[...]
    tr[...] = jnp.transpose(ids[...])
    for j in range(GROUPS):
        pieces = []
        for p in range(2):
            base = j * 32 + p * 16
            even = tr[pl.ds(base, SLOTS, stride=2), :]
            odd = tr[pl.ds(base + 1, SLOTS, stride=2), :]
            first = jnp.where(core == 0, even, odd)
            second = jnp.where(core == 0, odd, even)
            pieces.append(jnp.concatenate([first, second], axis=1))
        ids_out[pl.ds(j * SLOTS, SLOTS), 0, :] = jnp.where(parity == 0, pieces[0], pieces[1])
        ids_out[pl.ds(j * SLOTS, SLOTS), 1, :] = jnp.where(parity == 0, pieces[1], pieces[0])
    sub = lax.broadcasted_iota(jnp.int32, (8, PROJ), 0)
    used = jnp.full((8, PROJ), rows[core], jnp.int32)
    parts = jnp.where(sub == 0, jnp.right_shift(used, 4), jnp.bitwise_and(used, 15))
    table_out[pl.ds(VOCAB, 8), :] = parts.astype(F32).astype(BF16)
    row = lax.broadcasted_iota(jnp.int32, (EMB, PROJ), 0)
    weight = jnp.where(
        row < jnp.left_shift(jnp.int32(32), widths[core]), proj[core].astype(F32), 0.0
    ).astype(BF16)
    for c in loads:
        c.wait()
    store = pltpu.make_async_copy(packed, payload, sems.at[4])
    store.start()
    table_out[pl.ds(0, VOCAB), :] = jnp.dot(
        tab_buf[...], weight, preferred_element_type=F32
    ).astype(BF16)
    store.wait()


def prep(rows, widths, ids_t, tables, projections, user, down, deep, up):
    smem = pl.BlockSpec(memory_space=pltpu.SMEM)
    vmem = pl.BlockSpec(memory_space=pltpu.VMEM)
    hbm = pl.BlockSpec(memory_space=ANY)
    return pl.pallas_call(
        prep_kernel,
        out_shape=(
            jax.ShapeDtypeStruct((PEERS, 2, 2 * CAND), jnp.int32),
            jax.ShapeDtypeStruct((VOCAB + 8, PROJ), BF16),
            jax.ShapeDtypeStruct((PAYLOAD, 1024), BF16),
        ),
        in_specs=[smem, smem, vmem, hbm, vmem, vmem, hbm, hbm, hbm],
        out_specs=(vmem, vmem, hbm),
        scratch_shapes=[
            pltpu.VMEM((VOCAB, EMB), BF16),
            pltpu.VMEM((2 * CAND, CAND), jnp.int32),
            pltpu.VMEM((PAYLOAD, 1024), BF16),
            pltpu.SemaphoreType.DMA((5,)),
        ],
        name="prep",
    )(rows, widths, ids_t, tables, projections, user, down, deep, up)


def second_kernel(widths, tables, proj, table_out, tab_buf, sem):
    second = 1 - lax.axis_index("c")
    load = pltpu.make_async_copy(tables.at[second], tab_buf, sem)
    load.start()
    row = lax.broadcasted_iota(jnp.int32, (EMB, PROJ), 0)
    weight = jnp.where(
        row < jnp.left_shift(jnp.int32(32), widths[second]), proj[second].astype(F32), 0.0
    ).astype(BF16)
    load.wait()
    table_out[...] = jnp.dot(tab_buf[...], weight, preferred_element_type=F32).astype(BF16)


def second_table(widths, tables, projections):
    smem = pl.BlockSpec(memory_space=pltpu.SMEM)
    vmem = pl.BlockSpec(memory_space=pltpu.VMEM)
    hbm = pl.BlockSpec(memory_space=ANY)
    return pl.pallas_call(
        second_kernel,
        out_shape=pltpu.VMEM((VOCAB, PROJ), BF16),
        in_specs=[smem, hbm, vmem],
        out_specs=vmem,
        scratch_shapes=[pltpu.VMEM((VOCAB, EMB), BF16), pltpu.SemaphoreType.DMA],
        name="second_table",
    )(widths, tables, projections)


def lookup_kernel(rows, ids, own_a, own_b, other_a, other_b, out):
    core = lax.axis_index("c")
    lane = lax.broadcasted_iota(jnp.int32, (1, PROJ), 1)
    mine = jnp.where(lane < CAND, rows[core], rows[1 - core]).astype(F32)
    tails = [t[pl.ds(VOCAB, 8), :].astype(F32) for t in (other_a, other_b)]
    theirs = [t[0:1, :] * 16.0 + t[1:2, :] for t in tails]
    theirs = jnp.where(lane < CAND, theirs[0], theirs[1])
    lows, highs = [], []
    for q, used in enumerate((mine, theirs)):
        value = ids[:, q, :].astype(F32)
        quotient = jnp.floor(value / used)
        index = value - quotient * used
        index = jnp.where(index < 0.0, index + used, index)
        index = jnp.where(index >= used, index - used, index)
        high = jnp.floor(index * (1.0 / 256.0))
        lows.append(index - high * 256.0)
        highs.append(high)
    low = jnp.transpose(jnp.concatenate(lows, axis=0))
    high = jnp.transpose(jnp.concatenate(highs, axis=0))
    column = lax.broadcasted_iota(jnp.int32, (256, 256), 1).astype(F32)
    step = 256 // CAND
    for chunk in range(PEERS // step):
        acc = jnp.zeros((256, PROJ), F32)
        for q, pair in enumerate(((own_a, own_b), (other_a, other_b))):
            for k in range(2):
                spots = [q * PEERS + chunk * step + s for s in range(step)]
                lo = jnp.concatenate([low[k * CAND:(k + 1) * CAND, s:s + 1] for s in spots], axis=0)
                hi = jnp.concatenate([high[k * CAND:(k + 1) * CAND, s:s + 1] for s in spots], axis=0)
                for h in range(VOCAB // 256):
                    hot = jnp.where(lo + hi * 256.0 == column + h * 256.0, 1.0, 0.0).astype(BF16)
                    acc = acc + jnp.dot(
                        hot, pair[k][pl.ds(h * 256, 256), :], preferred_element_type=F32
                    )
        out[pl.ds(chunk * 256, 256), :] = acc.astype(BF16)


def lookup(rows, ids, own_a, own_b, other_a, other_b):
    vmem = pl.BlockSpec(memory_space=pltpu.VMEM)
    return pl.pallas_call(
        lookup_kernel,
        out_shape=jax.ShapeDtypeStruct((ROWS, PROJ), BF16),
        in_specs=[pl.BlockSpec(memory_space=pltpu.SMEM)] + [vmem] * 5,
        name="lookup",
    )(rows, in_vmem(ids), own_a, in_vmem(own_b), in_vmem(other_a), in_vmem(other_b))


def user_kernel(request, weight, packed, chosen, partial, w1_out, w2_out, feats, w1, sems):
    copies = [pltpu.make_async_copy(packed.at[:, pl.ds(256, 8), pl.ds(0, UIN)], feats, sems.at[0])]
    for n in range(8):
        where = w1 if n < 4 else w1_out
        copies.append(
            pltpu.make_async_copy(
                packed.at[n, pl.ds(0, 256), pl.ds(0, RANK + DEEP1)],
                where.at[pl.ds((n % 4) * 256, 256), :],
                sems.at[1 + n],
            )
        )
    for n in range(8):
        copies.append(
            pltpu.make_async_copy(
                packed.at[n, pl.ds(0, 256), pl.ds(RANK + DEEP1, 256)], w2_out.at[n], sems.at[9 + n]
            )
        )
    for c in copies:
        c.start()
    copies[0].wait()
    dense = feats[...].astype(F32)[:, 0, :].astype(BF16)
    pre = jnp.dot(dense, weight[...], preferred_element_type=F32)
    users = (pre * (1.0 / (1.0 + jnp.exp(-pre)))).astype(BF16)
    select = lax.broadcasted_iota(jnp.int32, (SLOTS, CAND), 0) == request[...]
    mine = lax.dot_general(
        jnp.where(select, 1.0, 0.0).astype(BF16), users, (((0,), (0,)), ((), ())),
        preferred_element_type=F32,
    ).astype(BF16)
    chosen[...] = mine
    for c in copies[1:]:
        c.wait()
    partial[...] = jnp.dot(mine, w1[...], preferred_element_type=F32)


def user_part(request, weight, packed):
    vmem = pl.BlockSpec(memory_space=pltpu.VMEM)
    hbm = pl.BlockSpec(memory_space=ANY)
    return pl.pallas_call(
        user_kernel,
        out_shape=(
            pltpu.VMEM((CAND, HALF), BF16),
            pltpu.VMEM((CAND, RANK + DEEP1), F32),
            pltpu.VMEM((HALF, RANK + DEEP1), BF16),
            pltpu.VMEM((8, RANK, 256), BF16),
        ),
        in_specs=[vmem, vmem, hbm],
        out_specs=(vmem, vmem, vmem, vmem),
        scratch_shapes=[
            pltpu.VMEM((8, 8, UIN), BF16),
            pltpu.VMEM((HALF, RANK + DEEP1), BF16),
            pltpu.SemaphoreType.DMA((17,)),
        ],
        name="user_part",
    )(request, weight, packed)


def dense_kernel(
    returned, w1, w2, chosen, partial, bias, mid, head_c, head_d, crossed_out, scores_out,
):
    slots = []
    for s in range(SLOTS):
        total = returned[s].astype(F32)
        for g in range(1, GROUPS):
            total = total + returned[g * SLOTS + s].astype(F32)
        slots.append(total.astype(BF16))
    item = jnp.concatenate(slots, axis=1)
    both = partial[...] + jnp.dot(item, w1[...], preferred_element_type=F32)
    low = both[:, :RANK].astype(BF16)
    deep = jnp.maximum(both[:, RANK:], 0.0).astype(BF16)
    hidden = jnp.maximum(jnp.dot(deep, mid[...], preferred_element_type=F32), 0.0)
    score = jnp.sum(hidden * head_d[...], axis=1, keepdims=True)
    for n in range(8):
        cols = slice(n * 256, (n + 1) * 256)
        upward = jnp.dot(low, w2[n], preferred_element_type=F32)
        base = (chosen[:, cols] if n < 4 else item[:, n * 256 - HALF:(n + 1) * 256 - HALF]).astype(F32)
        cross = (base * (upward + bias[:, cols]) + base).astype(BF16)
        crossed_out[:, cols] = cross
        score = score + jnp.sum(cross.astype(F32) * head_c[:, cols], axis=1, keepdims=True)
    scores_out[...] = jnp.transpose(jnp.broadcast_to(score, (CAND, 128)))[0:1, :]


def dense_part(returned, w1, w2, chosen, partial, *rest):
    vmem = pl.BlockSpec(memory_space=pltpu.VMEM)
    return pl.pallas_call(
        dense_kernel,
        out_shape=(
            jax.ShapeDtypeStruct((CAND, DENSE), BF16),
            jax.ShapeDtypeStruct((1, CAND), F32),
        ),
        in_specs=[vmem] * 9,
        name="dense_part",
    )(in_vmem(returned), in_vmem(w1), in_vmem(w2), in_vmem(chosen), in_vmem(partial), *rest)


def per_device(
    cand_ids,
    cand_request,
    tables,
    table_rows,
    width_choice,
    projections,
    user_dense,
    user_weight,
    cross_down,
    cross_up,
    cross_bias,
    deep_in,
    deep_mid,
    head_cross,
    head_deep,
):
    ids_out, own_a, payload = prep(
        table_rows, width_choice, cand_ids.T, tables, projections,
        user_dense, cross_down, deep_in, cross_up,
    )
    packed = lax.all_gather(payload, ("x", "c"), axis=0, tiled=True).reshape(8, PAYLOAD, 1024)
    other_a = lax.ppermute(own_a, "yp", [(0, 1), (1, 0)])
    received = lax.all_to_all(ids_out, ("yj", "z"), split_axis=0, concat_axis=0, tiled=True)
    widths, _ = lax.optimization_barrier((width_choice, ids_out))
    own_b = second_table(widths, tables, projections)
    other_b = lax.ppermute(other_a, "c", [(0, 1), (1, 0)])
    rows = lookup(table_rows, received, own_a, own_b, other_a, other_b)
    returned = lax.all_to_all(
        rows.reshape(PEERS, CAND, PROJ), ("yj", "z"), split_axis=0, concat_axis=0, tiled=True
    )
    chosen, partial, w1, w2 = user_part(cand_request.reshape(1, CAND), user_weight, packed)
    crossed, scores = dense_part(
        returned,
        w1,
        w2,
        chosen,
        partial,
        cross_bias.reshape(1, DENSE),
        deep_mid,
        head_cross.reshape(1, DENSE),
        head_deep.reshape(1, DEEP2),
    )
    return crossed, scores.reshape(CAND)


def solution(mesh):
    inner = Mesh(mesh.devices.reshape(GROUPS, 2, SLOTS, 4, 2), ("yj", "yp", "z", "x", "c"))
    wide = ("yj", "yp", "z")
    narrow = ("x", "c")
    everywhere = wide + narrow
    return jax.shard_map(
        per_device,
        mesh=inner,
        in_specs=(
            P(None, everywhere),
            P(everywhere),
            P(wide, None, None),
            P(wide),
            P(wide),
            P(wide, None, None),
            P(everywhere, None),
            P(),
            P(narrow, None),
            P(None, narrow),
            P(),
            P(narrow, None),
            P(),
            P(),
            P(),
        ),
        out_specs=(P(everywhere, None), P(everywhere)),
        check_vma=False,
    )
```

time: 101 us -> 90.8 us (0.90)
  blocking collectives: 27.4 us -> 0 us
  waiting for transfers between devices: 14 us -> 31.9 us
  starting transfers between devices: 7.72 us -> 25.3 us
  Pallas kernels: 33.9 us -> 19.1 us
  local copies, waits for them, and re-layouts: 1.62 us -> 0 us
  other arithmetic: 1.28 us -> 0 us
    all_to_all x1 -> x0, blocking collectives: 27.4 us -> none  [per_device(): lax.all_to_all(ids_out, ('yj', 'z'), split_axis=0, concat_axis=0, tiled=T...]
    all_to_all x0 -> x1, starting transfers between devices: none -> 16 us  [per_device(): lax.all_to_all(ids_out, ('yj', 'z'), split_axis=0, concat_axis=0, tiled=T...]
    pallas_call x2 -> x3, Pallas kernels: 22.6 us -> 10 us  [the longest x1 4.02 us: user_part(): pl.pallas_call(user_kernel, out_shape=(pltpu.VMEM((CAND, HALF), BF16), pl...]
    all_to_all x0 -> x1, waiting for transfers between devices: none -> 9.98 us  [per_device(): lax.all_to_all(ids_out, ('yj', 'z'), split_axis=0, concat_axis=0, tiled=T...]
    ppermute x1 -> x2, waiting for transfers between devices: 0.01 us -> 6.7 us  [the longest x1 6.7 us: per_device(): other_a = lax.ppermute(own_a, 'yp', [(0, 1), (1, 0)])]
    pallas_call x1, Pallas kernels: 4.44 us -> 2.42 us  [dense_part(): pl.pallas_call(dense_kernel, out_shape=(jax.ShapeDtypeStruct((CAND, DENSE...]
    ppermute x1 -> x2, starting transfers between devices: 3.48 us -> 5.39 us  [the longest x1 3.48 us: per_device(): other_a = lax.ppermute(own_a, 'yp', [(0, 1), (1, 0)])]
    unnamed x4 -> x0, local copies, waits for them, and re-layouts: 1.62 us -> none
  transfers between devices with their start and end apart: 3 -> 5, of which waited for: 1 -> 3; matrix products, arithmetic and copies ran while one was open for 0% -> 0% of each run, Pallas kernels for 11% -> 14%
where the time goes in v2:
time: 90.8 us; the launch traced here: 90.4 us
  waiting for transfers between devices  31.9 us (35%)
  starting transfers between devices  25.3 us (28%)
  Pallas kernels  19.1 us (21%)
  between operations  14.1 us (16%)
    all_to_all x1, starting transfers between devices, per_device(): lax.all_to_all(ids_out, ('yj', 'z'), split_axis=0, concat_axis=0, tiled=T...  16 us
    all_to_all x1, waiting for transfers between devices, per_device(): lax.all_to_all(rows.reshape(PEERS, CAND, PROJ), ('yj', 'z'), split_axis=0...  15.2 us
    all_to_all x1, waiting for transfers between devices, per_device(): lax.all_to_all(ids_out, ('yj', 'z'), split_axis=0, concat_axis=0, tiled=T...  9.98 us
    ppermute x1, waiting for transfers between devices, per_device(): other_a = lax.ppermute(own_a, 'yp', [(0, 1), (1, 0)])  6.7 us
    pallas_call x1, Pallas kernels, lookup(): pl.pallas_call(lookup_kernel, out_shape=jax.ShapeDtypeStruct((ROWS, PROJ)...  6.63 us
    pallas_call x1, Pallas kernels, user_part(): pl.pallas_call(user_kernel, out_shape=(pltpu.VMEM((CAND, HALF), BF16), pl...  4.02 us
    all_to_all x1, starting transfers between devices, per_device(): lax.all_to_all(rows.reshape(PEERS, CAND, PROJ), ('yj', 'z'), split_axis=0...  3.89 us
    pallas_call x1, Pallas kernels, prep(): pl.pallas_call(prep_kernel, out_shape=(jax.ShapeDtypeStruct((PEERS, 2, 2...  3.74 us
  transfers between devices with their start and end apart: 5, of which 3 were waited for; matrix products, arithmetic and copies ran while one was open for 0% of the time, Pallas kernels for 14%

profile of v2, /device:TPU:6, one launch (start us, length us, event | category | flops | bytes accessed | tf_op | source)
XLA Modules:
  0.0 90.4 jit_solution(15407903035329729809)
XLA Ops:
  7.2 0.0 all-gather.2.cloned.1.call-start
  7.2 3.7 %prep.1 = (s32[32,2,128]{2,1,0:T(2,128)}, bf16[1032,128]{1,0:T(8,128)(2,1)}, bf16[264,1024]{1,0:T(8,128)(2,1)}) custom-call(s32[2]{0:T(128)} %rows.3, s32[2]{0:T(128)} %widths.2, s32[64,128]{1,0:T(8,128)} %bitcast.10, bf16[2,1024,256]{2,1,0:T(8,128)(2,1)} %tables.3, bf16[2,256,128]{2,1,0:T(8,128)(2,1)} %proj.3, bf16[1,512]{1,0:T(2,128)(2,1)} %user.1, ...), custom_call_target="tpu_custom_call" | custom-call | tf_op jit(solution)/shard_map/prep/pallas_call | solution.py:83
  11.0 0.0 all-gather.2.cloned.1.call-update
  11.0 3.5 %collective-permute-start = (bf16[1032,128]{1,0:T(8,128)(2,1)}, bf16[1032,128]{1,0:T(8,128)(2,1)S(1)}, u32[]{:S(2)}, u32[]{:S(2)}) collective-permute-start(bf16[1032,128]{1,0:T(8,128)(2,1)} %get-tuple-element.13.own_a), channel_id=1, source_target_pairs={{0,64},{64,0},{1,65},{65,1},{2,66},{66,2},{3,67},{67,3},{4,68},{68... | collective-permute-start | bytes 792584 | tf_op jit(solution)/shard_map/ppermute | solution.py:290
  14.5 6.7 %collective-permute-done.other_a = bf16[1032,128]{1,0:T(8,128)(2,1)S(1)} collective-permute-done((bf16[1032,128]{1,0:T(8,128)(2,1)}, bf16[1032,128]{1,0:T(8,128)(2,1)S(1)}, u32[]{:S(2)}, u32[]{:S(2)}) %collective-permute-start) | collective-permute-done | bytes 264224 | tf_op jit(solution)/shard_map/ppermute | solution.py:290
  21.2 1.9 %collective-permute-start.1 = (bf16[1032,128]{1,0:T(8,128)(2,1)S(1)}, bf16[1032,128]{1,0:T(8,128)(2,1)S(1)}, u32[]{:S(2)}, u32[]{:S(2)}) collective-permute-start(bf16[1032,128]{1,0:T(8,128)(2,1)S(1)} %collective-permute-done.other_a), channel_id=1, source_target_pairs={{0,1},{1,0},{2,3},{3,2},{4,5},{5,4},{6,7},{7,6},{8,9},{9,8},{10,11... | collective-permute-start | bytes 792584 | tf_op jit(solution)/shard_map/ppermute | solution.py:294
  23.1 16.0 %all-to-all-start = ((s32[32,2,128]{2,1,0:T(2,128)}), s32[32,2,128]{2,1,0:T(2,128)S(1)}, u32[]{:S(2)}, u32[]{:S(2)}) async-start(s32[32,2,128]{2,1,0:T(2,128)} %get-tuple-element.12), calls=%async_computation | async-start | bytes 65536 | tf_op jit(solution)/shard_map/all_to_all | solution.py:291
  39.1 2.3 %second_table.1.own_b = bf16[1024,128]{1,0:T(8,128)(2,1)S(1)} custom-call(s32[2]{0:T(128)} %widths.2, bf16[2,1024,256]{2,1,0:T(8,128)(2,1)} %tables.3, bf16[2,256,128]{2,1,0:T(8,128)(2,1)} %proj.3), custom_call_target="tpu_custom_call" | custom-call | tf_op jit(solution)/shard_map/second_table/pallas_call | solution.py:118
  41.4 10.0 %all-to-all-done.ids = s32[32,2,128]{2,1,0:T(2,128)S(1)} async-done(((s32[32,2,128]{2,1,0:T(2,128)}), s32[32,2,128]{2,1,0:T(2,128)S(1)}, u32[]{:S(2)}, u32[]{:S(2)}) %all-to-all-start) | async-done | bytes 32800 | tf_op jit(solution)/shard_map/all_to_all | solution.py:291
  51.3 0.0 collective-permute-done.1.other_b
  51.3 6.6 %lookup.1 = bf16[2048,128]{1,0:T(8,128)(2,1)} custom-call(s32[2]{0:T(128)} %rows.3, s32[32,2,128]{2,1,0:T(2,128)S(1)} %all-to-all-done.ids, bf16[1032,128]{1,0:T(8,128)(2,1)} %get-tuple-element.13.own_a, bf16[1024,128]{1,0:T(8,128)(2,1)S(1)} %second_table.1.own_b, bf16[1032,128]{1,0:T(8,128)(2,1)S(1)} %collective-permute-done.other_a, ...), custom_call_target="tpu_custom_call" | custom-call | tf_op jit(solution)/shard_map/lookup/pallas_call | solution.py:166
  58.0 3.9 %all-to-all-start.1 = ((bf16[32,64,128]{2,1,0:T(8,128)(2,1)}), bf16[32,64,128]{2,1,0:T(8,128)(2,1)S(1)}, u32[]{:S(2)}, u32[]{:S(2)}) async-start(bf16[32,64,128]{2,1,0:T(8,128)(2,1)} %bitcast.9), calls=%async_computation.1 | async-start | bytes 1048576 | tf_op jit(solution)/shard_map/all_to_all | solution.py:296
  61.9 0.0 all-gather.2.cloned.1.call-done
  61.9 4.0 %user_part.1 = (bf16[64,1024]{1,0:T(8,128)(2,1)S(1)}, f32[64,768]{1,0:T(8,128)S(1)}, bf16[1024,768]{1,0:T(8,128)(2,1)S(1)}, bf16[8,256,256]{2,1,0:T(8,128)(2,1)S(1)}) custom-call(s32[1,64]{1,0:T(1,128)} %bitcast.14, bf16[512,1024]{1,0:T(8,128)(2,1)} %weight.1, bf16[8,264,1024]{2,1,0:T(8,128)(2,1)} %bitcast.8), custom_call_target="tpu_custom_call" | custom-call | tf_op jit(solution)/shard_map/user_part/pallas_call | solution.py:211
  65.9 15.2 %all-to-all-done.1.returned = bf16[32,64,128]{2,1,0:T(8,128)(2,1)S(1)} async-done(((bf16[32,64,128]{2,1,0:T(8,128)(2,1)}), bf16[32,64,128]{2,1,0:T(8,128)(2,1)S(1)}, u32[]{:S(2)}, u32[]{:S(2)}) %all-to-all-start.1) | async-done | bytes 524320 | tf_op jit(solution)/shard_map/all_to_all | solution.py:296
  81.1 2.4 %dense_part.1 = (bf16[64,2048]{1,0:T(8,128)(2,1)}, f32[1,64]{1,0:T(1,128)}) custom-call(bf16[32,64,128]{2,1,0:T(8,128)(2,1)S(1)} %all-to-all-done.1.returned, bf16[1024,768]{1,0:T(8,128)(2,1)S(1)} %get-tuple-element.16.w1, bf16[8,256,256]{2,1,0:T(8,128)(2,1)S(1)} %get-tuple-element.17.w2, bf16[64,1024]{1,0:T(8,128)(2,1)S(1)} %get-tuple-element.18.chosen, ...), custom_call_target="tpu_custom_call" | custom-call | tf_op jit(solution)/shard_map/dense_part/pallas_call | solution.py:257
Async XLA Ops:
  7.2 54.7 %all-gather.2.cloned.1.call-start = ((), (), s32[]{:S(2)}) async-start(), calls=%async_computation.2 | async-start | bytes 4866048 | tf_op jit(solution)/shard_map/all_gather | solution.py:289
  11.0 10.2 %collective-permute-start = (bf16[1032,128]{1,0:T(8,128)(2,1)}, bf16[1032,128]{1,0:T(8,128)(2,1)S(1)}, u32[]{:S(2)}, u32[]{:S(2)}) collective-permute-start(bf16[1032,128]{1,0:T(8,128)(2,1)} %get-tuple-element.13.own_a), channel_id=1, source_target_pairs={{0,64},{64,0},{1,65},{65,1},{2,66},{66,2},{3,67},{67,3},{4,68},{68... | collective-permute-start | bytes 792584 | tf_op jit(solution)/shard_map/ppermute | solution.py:290
  21.2 30.2 %collective-permute-start.1 = (bf16[1032,128]{1,0:T(8,128)(2,1)S(1)}, bf16[1032,128]{1,0:T(8,128)(2,1)S(1)}, u32[]{:S(2)}, u32[]{:S(2)}) collective-permute-start(bf16[1032,128]{1,0:T(8,128)(2,1)S(1)} %collective-permute-done.other_a), channel_id=1, source_target_pairs={{0,1},{1,0},{2,3},{3,2},{4,5},{5,4},{6,7},{7,6},{8,9},{9,8},{10,11... | collective-permute-start | bytes 792584 | tf_op jit(solution)/shard_map/ppermute | solution.py:294
  23.1 28.2 %all-to-all-start = ((s32[32,2,128]{2,1,0:T(2,128)}), s32[32,2,128]{2,1,0:T(2,128)S(1)}, u32[]{:S(2)}, u32[]{:S(2)}) async-start(s32[32,2,128]{2,1,0:T(2,128)} %get-tuple-element.12), calls=%async_computation | async-start | bytes 65536 | tf_op jit(solution)/shard_map/all_to_all | solution.py:291
  58.0 23.1 %all-to-all-start.1 = ((bf16[32,64,128]{2,1,0:T(8,128)(2,1)}), bf16[32,64,128]{2,1,0:T(8,128)(2,1)S(1)}, u32[]{:S(2)}, u32[]{:S(2)}) async-start(bf16[32,64,128]{2,1,0:T(8,128)(2,1)} %bitcast.9), calls=%async_computation.1 | async-start | bytes 1048576 | tf_op jit(solution)/shard_map/all_to_all | solution.py:296
Sparse Core Ops, SparseCore 0:
  11.1 40.7 all-gather.1
